TPU v7x, 32 devices: a whole 2x2x4 slice. The times are simulated.
32 devices in a mesh: groups: 2 (over y), expert: 4 (over z), dp: 4 (over x, core).
Axes of the slice: x: 2, y: 2, z: 4, core: 2. Of those that a mesh axis runs over, the one named last changes fastest.
Arguments:
- tokens: bfloat16 [512, 6144], P(('groups', 'expert'), 'dp'), parts along dimension 0, may hold values from -6 to 6
- expert_ids: int32 [512, 8], P(('groups', 'expert')), parts along dimension 0, may hold values from 0 to 31, all different within a row; in each aligned block of 64 rows (0 to 63, 64 to 127, ...) at most 32 rows name the same one
- scores: float32 [512, 8], P(('groups', 'expert')), parts along dimension 0, may hold values from -8 to 8
- w_gate: bfloat16 [32, 6144, 1024], P('expert', 'dp'), may hold values from -0.078125 to 0.078125
- w_up: bfloat16 [32, 6144, 1024], P('expert', 'dp'), may hold values from -0.078125 to 0.078125
- w_down: bfloat16 [32, 1024, 6144], P('expert', None, 'dp'), may hold values from -0.1875 to 0.1875
Outputs:
- mixed: bfloat16 [512, 6144], P(('groups', 'expert'), 'dp'), parts along dimension 0
There are 2 independent parts, one for each index of `groups`. A program takes and returns all parts, laid end to end along the dimension named above; an argument that names none is the same for every part. Nothing has to cross between parts.
Inputs may be any that keep to these rules, and one draw needn't show every extreme that they name: `expert_ids`: each row names 8 different experts; among the rows of one index of expert (aligned blocks of 64 rows) no expert is named by more than 32 rows, a bound that some block reaches.
All inputs are finite; a program needn't handle non-finite values.
Results may differ from a plain program's by a relative error of at most 0.024.
Values may be sent and summed in bfloat16 or wider, within the bound.
A program may use at most 128 MiB of HBM per device.

v0:
```python
import functools

import jax
import jax.numpy as jnp
from jax import lax
from jax.experimental import pallas as pl
from jax.experimental.pallas import tpu as pltpu
from jax.sharding import PartitionSpec as P

MESH = pl.DeviceIdType.MESH
F32, BF16 = jnp.float32, jnp.bfloat16
LAGS = (0, 1, 3, 5, 7)


def dot(a, b, dims=((1,), (0,))):
    return lax.dot_general(a, b, (dims, ((), ())), preferred_element_type=F32)


def remote(src, dst, send, recv, **where):
    return pltpu.make_async_remote_copy(
        src_ref=src, dst_ref=dst, send_sem=send, recv_sem=recv,
        device_id=where, device_id_type=MESH,
    )


def tile_of(size):
    for tile in (512, 384, 256, 128):
        if size % tile == 0:
            return tile
    return size


def kernel(dims, tok_ref, ids_ref, sco_ref, wg_hbm, wu_hbm, wd_hbm, out_ref,
           wg, wu, wd, xall, meta, slot_c, wgt_c, rows, s1, r1, keep, s2, r2, hid, acc,
           rs_s, rs_r, rs_l,
           wsem, ag_s, ag_r, p_s, p_r, q_s, q_r, h_s, h_r, f_s, f_r, t_s, t_r):
    E, DP, EL, NCH, G, CAP, NB, HALF, CT, tw = dims
    M = DP // 2
    tok, width = tok_ref.shape
    H = wg.shape[2]
    hb = H // DP
    R, T = G * CAP, G * tok
    N = EL * NCH
    ct = CT
    chunks = range(width // tw)
    n_items = N + 2 * HALF
    e = lax.axis_index("expert")
    d = lax.axis_index("dp")
    x, c = lax.div(d, 2), lax.rem(d, 2)
    mate = 2 * x + 1 - c
    has_left, has_right = e > 0, e < E - 1

    def place(s):
        return lax.rem(s + E // 4, E)

    def across(k):
        return lax.rem(x + k, M)

    def source(k):
        return lax.rem(x + M - k, M)

    def w_gu(j, slot):
        return (pltpu.make_async_copy(wg_hbm.at[j], wg.at[slot], wsem.at[0, slot]),
                pltpu.make_async_copy(wu_hbm.at[j], wu.at[slot], wsem.at[1, slot]))

    def w_d(j, slot):
        return pltpu.make_async_copy(wd_hbm.at[j], wd.at[slot], wsem.at[2, slot])

    for j in range(NB):
        for copy in w_gu(j, j):
            copy.start()
    for j in range(NB):
        w_d(j, j).start()

    barrier = pltpu.get_barrier_semaphore()

    @pl.when(has_left)
    def _():
        pl.semaphore_signal(barrier, inc=1, device_id={"expert": e - 1}, device_id_type=MESH)

    @pl.when(has_right)
    def _():
        pl.semaphore_signal(barrier, inc=1, device_id={"expert": e + 1}, device_id_type=MESH)

    pl.semaphore_signal(barrier, inc=1, device_id={"dp": mate}, device_id_type=MESH)
    for k in range(1, M):
        pl.semaphore_signal(
            barrier, inc=1, device_id={"dp": 2 * across(k) + c}, device_id_type=MESH)

    n_exp = E * EL
    affinity = 1.0 / (1.0 + jnp.exp(-sco_ref[...]))
    weights = 2.5 * affinity / jnp.sum(affinity, axis=0, keepdims=True)
    number = lax.broadcasted_iota(jnp.int32, (n_exp, tok), 0)
    routed = jnp.zeros((n_exp, tok), F32)
    weight = jnp.zeros((n_exp, tok), F32)
    for k in range(ids_ref.shape[0]):
        hit = ids_ref[k:k + 1, :] == number
        routed = routed + jnp.where(hit, 1.0, 0.0)
        weight = weight + jnp.where(hit, weights[k:k + 1, :], 0.0)
    earlier = (lax.broadcasted_iota(jnp.int32, (tok, tok), 0)
               < lax.broadcasted_iota(jnp.int32, (tok, tok), 1))
    rank = dot(routed.astype(BF16), jnp.where(earlier, 1.0, 0.0).astype(BF16))
    base = (place(e) * CAP).astype(F32)
    meta[e, :, :tok] = jnp.where(routed > 0.5, rank + base, -1.0)
    meta[e, :, tok:] = weight
    xall[place(e)] = tok_ref[...]

    pl.semaphore_wait(barrier, M + has_left.astype(jnp.int32) + has_right.astype(jnp.int32))

    def gather_to(s, side, target):
        return (remote(meta.at[s], meta.at[s], ag_s.at[side, 0, s], ag_r.at[0, s], expert=target),
                remote(xall.at[place(s)], xall.at[place(s)], ag_s.at[side, 1, s], ag_r.at[1, s], expert=target))

    def start_right(s):
        @pl.when(has_right)
        def _():
            for copy in gather_to(s, 0, e + 1):
                copy.start()

    def start_left(s):
        @pl.when(has_left)
        def _():
            for copy in gather_to(s, 1, e - 1):
                copy.start()

    start_right(e)
    start_left(e)

    def gather_step(k, carry):
        @pl.when(e - k >= 0)
        def _():
            for copy in gather_to(e - k, 0, e):
                copy.wait_recv()
            start_right(e - k)

        @pl.when(e + k <= E - 1)
        def _():
            for copy in gather_to(e + k, 1, e):
                copy.wait_recv()
            start_left(e + k)

        return carry

    def list_slots(places):
        for p in places:
            own = meta[(p + E - E // 4) % E, pl.ds(e * EL, EL), :]
            lanes = slice(p % 2 * tok, (p % 2 + 1) * tok)
            slot_c[p // 2, :, lanes] = own[:, :tok]
            wgt_c[p // 2, :, lanes] = own[:, tok:]

    if HALF:
        lax.fori_loop(1, 3 * E // 4, gather_step, 0)
        list_slots(range(E // 2, E))
    else:
        lax.fori_loop(1, E, gather_step, 0)
        list_slots(range(E))
    acc[...] = jnp.zeros_like(acc)

    class Item:
        def __init__(self, j, q, parts, first, last):
            self.j, self.q, self.first, self.last = j, q, first, last
            self.group = G // parts
            self.rows, self.toks = R // parts, T // parts
            self.start = q * self.group
            if parts == 1:
                self.buf = j if NCH == 1 else j * NCH + q
                self.sem = 2 * self.buf
                self.span = pl.ds(0, R)
            else:
                self.buf, self.sem = j, 2 * j + q
                self.span = pl.ds(pl.multiple_of(q * self.rows, self.rows), self.rows)
            self.places = pl.ds(self.start, self.group)

        def row(self, table):
            pairs = self.group // 2
            return jnp.concatenate(
                [table[self.q * pairs + p, pl.ds(self.j, 1), :] for p in range(pairs)], axis=1)

    def taken(it):
        row = it.row(slot_c)
        first = it.start * CAP
        return (row.astype(jnp.int32) - first
                == lax.broadcasted_iota(jnp.int32, (it.rows, it.toks), 0))

    def pair_copy(it):
        return remote(s1.at[it.buf, :, it.span], r1.at[it.buf, :, it.span],
                      p_s.at[it.sem], p_r.at[it.sem], dp=mate)

    def sum_copy(it, k):
        return remote(s2.at[it.buf, across(k), it.span], r2.at[it.buf, x, it.span],
                      q_s.at[it.sem, k], q_r.at[it.sem, k], dp=2 * across(k) + c)

    def share_copy(it, k):
        return remote(hid.at[it.buf, d, it.span], hid.at[it.buf, d, it.span],
                      h_s.at[it.sem, k], h_r.at[it.sem, k], dp=2 * across(k) + c)

    def mate_copy(it, k):
        block = 2 * source(k) + c
        return remote(hid.at[it.buf, block, it.span], hid.at[it.buf, block, it.span],
                      f_s.at[it.sem, k], f_r.at[it.sem, k], dp=mate)

    def stage_a(it):
        j, span = it.j, it.span
        slot = lax.rem(j, NB)

        @pl.when(it.first)
        def _():
            for copy in w_gu(j, slot):
                copy.wait()

        pick = jnp.where(taken(it), 1.0, 0.0).astype(BF16)
        for at in range(0, width, ct):
            xq = xall[it.places, :, at:at + ct].reshape(it.toks, ct)
            rows[:it.rows, at:at + ct] = dot(pick, xq).astype(BF16)

        def block(m, core):
            cols = pl.ds(pl.multiple_of((2 * m + core) * hb, hb), hb)
            xr = rows[:it.rows, :]
            return dot(xr, wg[slot, :, cols]), dot(xr, wu[slot, :, cols])

        for m in range(M):
            g, u = block(m, 1 - c)
            s1[it.buf, m, span, :hb] = g.astype(BF16)
            s1[it.buf, m, span, hb:] = u.astype(BF16)
        pair_copy(it).start()
        for m in range(M):
            g, u = block(m, c)
            keep[it.buf, m, span, :hb] = g
            keep[it.buf, m, span, hb:] = u

        @pl.when(it.last & (j + NB < EL))
        def _():
            for copy in w_gu(j + NB, slot):
                copy.start()

    def stage_b(it):
        i, span = it.buf, it.span
        pair_copy(it).wait_recv()
        for k in range(1, M):
            to = across(k)
            s2[i, to, span] = (keep[i, to, span] + r1[i, to, span].astype(F32)).astype(BF16)
            sum_copy(it, k).start()
        keep[i, x, span] = keep[i, x, span] + r1[i, x, span].astype(F32)

    def stage_c(it):
        i, span = it.buf, it.span
        total = keep[i, x, span]
        for k in range(1, M):
            sum_copy(it, k).wait_recv()
            total = total + r2[i, source(k), span].astype(F32)
        g, u = total[:, :hb], total[:, hb:]
        hid[i, d, span] = (g / (1.0 + jnp.exp(-g)) * u).astype(BF16)
        for k in range(1, M):
            share_copy(it, k).start()
        mate_copy(it, 0).start()

    def stage_d(it):
        for k in range(1, M):
            share_copy(it, k).wait_recv()
            mate_copy(it, k).start()

    def stage_e(it):
        j, span = it.j, it.span
        slot = lax.rem(j, NB)

        @pl.when(it.first)
        def _():
            w_d(j, slot).wait()

        for k in range(M):
            mate_copy(it, k).wait_recv()
        hit = taken(it)
        scale = jnp.sum(jnp.where(hit, it.row(wgt_c), 0.0),
                        axis=1, keepdims=True)
        pick = jnp.where(hit, 1.0, 0.0).astype(BF16)
        hidden = jnp.concatenate([hid[it.buf, b, span] for b in range(DP)], axis=1)
        for at in range(0, width, ct):
            out = (dot(hidden, wd[slot, :, at:at + ct]) * scale).astype(BF16)
            add = dot(pick, out, ((0,), (0,))).reshape(it.group, tok, ct)
            acc[it.places, :, at:at + ct] += add

        @pl.when(it.last & (j + NB < EL))
        def _():
            w_d(j + NB, slot).start()

    def tail_right(s, n, target):
        return remote(rs_s.at[s, n], rs_r.at[s, n], t_s.at[s, n], t_r.at[0, s, n], expert=target)

    def tail_left(s, n, target):
        return remote(rs_s.at[s, n], rs_l.at[s, n], t_s.at[s, n], t_r.at[1, s, n], expert=target)

    def first_sums(s, copy_to, target):
        for n in chunks:
            rs_s[s, n] = acc[place(s), :, n * tw:(n + 1) * tw].astype(BF16)
            copy_to(s, n, target).start()

    def outer_sums():
        @pl.when(jnp.logical_not(has_left))
        def _():
            first_sums(E - 1, tail_right, e + 1)

        @pl.when(jnp.logical_not(has_right))
        def _():
            first_sums(0, tail_left, e - 1)

    stages = (stage_a, stage_b, stage_c, stage_d, stage_e)

    n_ends = n_items - 2 * HALF

    def on_item(t, stage):
        if HALF == 0:
            if NCH == 1:
                stage(Item(t, 0, 1, t >= 0, t >= 0))
            else:
                q = lax.rem(t, NCH)
                stage(Item(lax.div(t, NCH), q, 1, q == 0, q == NCH - 1))
            return
        in_full = (t >= 2 * HALF) & (t < n_ends)

        @pl.when(in_full)
        def _():
            stage(Item(t - HALF, 0, 1, t >= 0, t >= 0))

        @pl.when(jnp.logical_not(in_full))
        def _():
            end = lax.div(t, n_ends)
            u = t - end * n_ends
            turn = lax.div(u, HALF)
            j = lax.rem(u, HALF) + end * (EL - HALF)
            q = end * turn + (1 - end) * (1 - turn)
            stage(Item(j, q, 2, turn == 0, turn == 1))

    def step(i, carry):
        if HALF:
            @pl.when(i == HALF)
            def _():
                lax.fori_loop(3 * E // 4, E, gather_step, 0)
                list_slots(range(E // 2))

        for stage, lag in zip(stages, LAGS):
            @pl.when((i >= lag) & (i < n_items + lag))
            def _(stage=stage, lag=lag):
                on_item(i - lag, stage)
        if HALF:
            @pl.when(i == n_items - HALF - 1 + LAGS[-1])
            def _():
                outer_sums()
        return carry

    lax.fori_loop(0, n_items + LAGS[-1], step, 0)

    if not HALF:
        outer_sums()

    def tail_step(t, carry):
        far, near = E - 1 - t, t
        for n in chunks:
            cols = slice(n * tw, (n + 1) * tw)

            @pl.when((far > e) & has_left)
            def _():
                tail_right(far, n, e).wait_recv()
                rs_s[far, n] = (acc[place(far), :, cols] + rs_r[far, n].astype(F32)).astype(BF16)
                tail_right(far, n, e + 1).start()

            @pl.when((far > e) & jnp.logical_not(has_left) & (t > 0))
            def _():
                rs_s[far, n] = acc[place(far), :, cols].astype(BF16)
                tail_right(far, n, e + 1).start()

            @pl.when((near < e) & has_right)
            def _():
                tail_left(near, n, e).wait_recv()
                rs_s[near, n] = (acc[place(near), :, cols]
                                 + rs_l[near, n].astype(F32)).astype(BF16)
                tail_left(near, n, e - 1).start()

            @pl.when((near < e) & jnp.logical_not(has_right) & (t > 0))
            def _():
                rs_s[near, n] = acc[place(near), :, cols].astype(BF16)
                tail_left(near, n, e - 1).start()

        return carry

    lax.fori_loop(0, E - 1, tail_step, 0)

    for n in chunks:
        cols = slice(n * tw, (n + 1) * tw)

        @pl.when(has_left)
        def _():
            tail_right(e, n, e).wait_recv()
            acc[place(e), :, cols] = acc[place(e), :, cols] + rs_r[e, n].astype(F32)

        @pl.when(has_right)
        def _():
            tail_left(e, n, e).wait_recv()
            acc[place(e), :, cols] = acc[place(e), :, cols] + rs_l[e, n].astype(F32)

        out_ref[:, cols] = acc[place(e), :, cols].astype(BF16)

    def drain_line(s, carry):
        @pl.when((s <= e) & has_right)
        def _():
            for copy in gather_to(s, 0, e):
                copy.wait_send()

        @pl.when((s >= e) & has_left)
        def _():
            for copy in gather_to(s, 1, e):
                copy.wait_send()

        @pl.when(s != e)
        def _():
            for n in chunks:
                tail_right(s, n, e).wait_send()

        return carry

    lax.fori_loop(0, E, drain_line, 0)

    def drain(it):
        pair_copy(it).wait_send()
        mate_copy(it, 0).wait_send()
        for k in range(1, M):
            sum_copy(it, k).wait_send()
            share_copy(it, k).wait_send()
            mate_copy(it, k).wait_send()

    def drain_item(t, carry):
        on_item(t, drain)
        return carry

    lax.fori_loop(0, n_items, drain_item, 0)


def on_device(tokens, expert_ids, scores, w_gate, w_up, w_down):
    E, DP = lax.axis_size("expert"), lax.axis_size("dp")
    tok, width = tokens.shape
    top = expert_ids.shape[1]
    EL, _, H = w_gate.shape
    n_exp = E * EL
    CAP = 2 * tok * top // n_exp
    G = min(E, 4)
    NCH = E // G
    NB = min(3, EL)
    HALF = 2 if NCH == 1 and G == 4 and EL > 4 else 0
    ct = tile_of(width)
    tw = width
    tail = (E, width // tw, tok, tw)
    M, hb, R, N = DP // 2, H // DP, G * CAP, EL * NCH
    vmem, dma = pltpu.VMEM, pltpu.SemaphoreType.DMA
    scratch = [
        vmem((NB, width, H), BF16), vmem((NB, width, H), BF16), vmem((NB, H, width), BF16),
        vmem((E, tok, width), BF16), vmem((E, n_exp, 2 * tok), F32),
        vmem((E // 2, EL, 2 * tok), F32), vmem((E // 2, EL, 2 * tok), F32),
        vmem((R, width), BF16),
        vmem((N, M, R, 2 * hb), BF16), vmem((N, M, R, 2 * hb), BF16),
        vmem((N, M, R, 2 * hb), F32),
        vmem((N, M, R, 2 * hb), BF16), vmem((N, M, R, 2 * hb), BF16),
        vmem((N, DP, R, hb), BF16),
        vmem((E, tok, width), F32),
        vmem(tail, BF16), vmem(tail, BF16), vmem(tail, BF16),
        dma((3, NB)), dma((2, 2, E)), dma((2, E)),
        dma((2 * N,)), dma((2 * N,)), dma((2 * N, M)), dma((2 * N, M)), dma((2 * N, M)),
        dma((2 * N, M)), dma((2 * N, M)), dma((2 * N, M)),
        dma((E, width // tw)), dma((2, E, width // tw)),
    ]
    whole = pl.BlockSpec(memory_space=pltpu.VMEM)
    hbm = pl.BlockSpec(memory_space=pl.ANY)
    return pl.pallas_call(
        functools.partial(kernel, (E, DP, EL, NCH, G, CAP, NB, HALF, ct, tw)),
        out_shape=jax.ShapeDtypeStruct((tok, width), BF16),
        in_specs=[whole] * 3 + [hbm] * 3,
        out_specs=whole,
        scratch_shapes=scratch,
        compiler_params=pltpu.CompilerParams(
            collective_id=0, has_side_effects=True, vmem_limit_bytes=60 * 2**20),
        name="routed_experts",
    )(tokens, expert_ids.T, scores.T, w_gate, w_up, w_down)


def solution(mesh):
    in_specs = (
        P(("groups", "expert"), "dp"),
        P(("groups", "expert"), None),
        P(("groups", "expert"), None),
        P("expert", "dp", None),
        P("expert", "dp", None),
        P("expert", None, "dp"),
    )
    out_specs = P(("groups", "expert"), "dp")
    return jax.shard_map(
        on_device, mesh=mesh, in_specs=in_specs, out_specs=out_specs, check_vma=False
    )
```

profile of v0, /device:TPU:0, one launch (start us, length us, event | category | flops | bytes accessed | tf_op | source)
XLA Modules:
  0.0 86.9 jit_solution(13508919637118717366)
XLA Ops:
  0.0 85.3 %routed_experts.1 = bf16[64,1536]{1,0:T(8,128)(2,1)} custom-call(bf16[64,1536]{1,0:T(8,128)(2,1)} %tok_ref.1, s32[8,64]{1,0:T(8,128)} %bitcast.2, f32[8,64]{1,0:T(8,128)} %bitcast.3, bf16[8,1536,1024]{2,1,0:T(8,128)(2,1)} %wg_hbm.1, bf16[8,1536,1024]{2,1,0:T(8,128)(2,1)} %wu_hbm.1, bf16[8,1024,1536]{2,1,0:T(8,128)(2,1)} %wd_hbm.1), custom_call_target="tpu_custom_call" | custom-call | tf_op jit(solution)/shard_map/routed_experts/pallas_call | solution.py:471
  85.3 1.6 %copy.8 = bf16[64,1536]{1,0:T(8,128)(2,1)} copy(bf16[64,1536]{1,0:T(8,128)(2,1)} %routed_experts.1) | data formatting | bytes 393216
where the time goes:
time: 87.1 us; the launch traced here: 86.9 us
  Pallas kernels  85.3 us (98%)
  local copies, waits for them, and re-layouts  1.62 us (2%)
    pallas_call x1, Pallas kernels, on_device(): pl.pallas_call(functools.partial(kernel, (E, DP, EL, NCH, G, CAP, NB, HAL...  85.3 us

commit v1 on v0

v1 whole, which is shorter than its diff:
```python
import functools

import jax
import jax.numpy as jnp
from jax import lax
from jax.experimental import pallas as pl
from jax.experimental.pallas import tpu as pltpu
from jax.sharding import PartitionSpec as P

MESH = pl.DeviceIdType.MESH
F32, BF16 = jnp.float32, jnp.bfloat16
LAGS = (0, 1, 3, 5, 7)
LINE_LAGS = (0, 1, 3, 5, 6)


def dot(a, b, dims=((1,), (0,))):
    return lax.dot_general(a, b, (dims, ((), ())), preferred_element_type=F32)


def remote(src, dst, send, recv, **where):
    return pltpu.make_async_remote_copy(
        src_ref=src, dst_ref=dst, send_sem=send, recv_sem=recv,
        device_id=where, device_id_type=MESH,
    )


def tile_of(size):
    for tile in (512, 384, 256, 128):
        if size % tile == 0:
            return tile
    return size


def kernel(dims, tok_ref, ids_ref, sco_ref, wg_hbm, wu_hbm, wd_hbm, out_ref,
           wg, wu, wd, xall, route, slot_c, wgt_c, rows, s1, r1, keep, s2, r2, hid, acc,
           rs_s, rs_in,
           wsem, dsem, ag_s, ag_r, p_s, p_r, q_s, q_r, h_s, h_r, f_r, t_s, t_r):
    E, DP, EL, NCH, G, CAP, NB, ND, LINE, ct = dims
    M = DP // 2
    tok, width = tok_ref.shape
    top = ids_ref.shape[0]
    H = wg.shape[2]
    hb = H // DP
    R, T = G * CAP, G * tok
    N = EL * NCH
    K = EL // 2
    half = tok // 2
    EP = slot_c.shape[1]
    e = lax.axis_index("expert")
    d = lax.axis_index("dp")
    x, c = lax.div(d, 2), lax.rem(d, 2)
    mate = 2 * x + 1 - c
    has_left, has_right = e > 0, e < E - 1
    if LINE:
        low = e < 2
        mid = (e == 1) | (e == 2)
        onward = jnp.where(low, 0, 1)
        nb = jnp.where(low, e + 1, e - 1)
        fb = jnp.where(low, 3, 0)
        fa = 6 - e - nb - fb
        order = (e, nb, fa, fb)

    def across(k):
        return lax.rem(x + k, M)

    def source(k):
        return lax.rem(x + M - k, M)

    def w_gu(j, slot):
        return (pltpu.make_async_copy(wg_hbm.at[j], wg.at[slot], wsem.at[0, slot]),
                pltpu.make_async_copy(wu_hbm.at[j], wu.at[slot], wsem.at[1, slot]))

    def w_d(j, slot):
        return pltpu.make_async_copy(wd_hbm.at[j], wd.at[slot], dsem.at[slot])

    def start_down():
        for j in range(ND):
            w_d(j, j).start()

    for j in range(NB):
        for copy in w_gu(j, j):
            copy.start()
    if not LINE:
        start_down()

    barrier = pltpu.get_barrier_semaphore()

    @pl.when(has_left)
    def _():
        pl.semaphore_signal(barrier, inc=1, device_id={"expert": e - 1}, device_id_type=MESH)

    @pl.when(has_right)
    def _():
        pl.semaphore_signal(barrier, inc=1, device_id={"expert": e + 1}, device_id_type=MESH)

    pl.semaphore_signal(barrier, inc=1, device_id={"dp": mate}, device_id_type=MESH)
    for k in range(1, M):
        pl.semaphore_signal(
            barrier, inc=1, device_id={"dp": 2 * across(k) + c}, device_id_type=MESH)

    route[e, :top] = ids_ref[...].astype(F32)
    route[e, top:] = sco_ref[...]
    xall[e] = tok_ref[...]

    def routing(block, pair, side):
        affinity = 1.0 / (1.0 + jnp.exp(-route[block, top:]))
        weights = 2.5 * affinity / jnp.sum(affinity, axis=0, keepdims=True)
        number = lax.broadcasted_iota(jnp.int32, (EP, tok), 0) + e * EL
        number = number.astype(F32)
        routed = jnp.zeros((EP, tok), F32)
        weight = jnp.zeros((EP, tok), F32)
        for k in range(top):
            hit = route[block, k:k + 1] == number
            routed = routed + jnp.where(hit, 1.0, 0.0)
            weight = weight + jnp.where(hit, weights[k:k + 1, :], 0.0)
        earlier = (lax.broadcasted_iota(jnp.int32, (tok, tok), 0)
                   < lax.broadcasted_iota(jnp.int32, (tok, tok), 1))
        rank = dot(routed.astype(BF16), jnp.where(earlier, 1.0, 0.0).astype(BF16))
        first = jnp.asarray((2 * pair + side) * CAP, F32)
        lanes = slice(side * tok, (side + 1) * tok)
        slot_c[pair, :, lanes] = jnp.where(routed > 0.5, rank + first, -1.0)
        wgt_c[pair, :, lanes] = weight

    acc[...] = jnp.zeros_like(acc)
    if LINE:
        routing(e, 0, 0)

    with jax.named_scope("barrierw"):
        pl.semaphore_wait(barrier, M + has_left.astype(jnp.int32) + has_right.astype(jnp.int32))

    def gather_to(s, side, target, parts=(0, 1, 2)):
        copies = []
        for p in parts:
            ref = route.at[s] if p == 0 else xall.at[s, pl.ds((p - 1) * half, half)]
            copies.append(remote(ref, ref, ag_s.at[side, p, s], ag_r.at[p, s], expert=target))
        return copies

    def start_right(s, parts=(0, 1, 2)):
        @pl.when(has_right)
        def _():
            for copy in gather_to(s, 0, e + 1, parts):
                copy.start()

    def start_left(s, parts=(0, 1, 2)):
        @pl.when(has_left)
        def _():
            for copy in gather_to(s, 1, e - 1, parts):
                copy.start()

    def gather_step(k, parts=(0, 1, 2)):
        @pl.when(e - k >= 0)
        def _():
            for copy in gather_to(e - k, 0, e, parts):
                copy.wait_recv()
            start_right(e - k, parts)

        @pl.when(e + k <= E - 1)
        def _():
            for copy in gather_to(e + k, 1, e, parts):
                copy.wait_recv()
            start_left(e + k, parts)

    def arrived(s, parts=(0, 1, 2)):
        for copy in gather_to(s, 0, e, parts):
            copy.wait_recv()

    for parts in ((0, 1), (2,)):
        start_right(e, parts)
        start_left(e, parts)

    if LINE:
        with jax.named_scope("gather1"):
            for parts in ((0, 1), (2,)):
                gather_step(1, parts)
            routing(nb, 0, 1)
    else:
        def whole_step(k, carry):
            gather_step(k)
            return carry

        def list_pair(p, carry):
            routing(2 * p, p, 0)
            routing(2 * p + 1, p, 1)
            return carry

        lax.fori_loop(1, E, whole_step, 0)
        lax.fori_loop(0, E // 2, list_pair, 0)

    class Item:
        def __init__(self, j, q, parts):
            self.j, self.q, self.parts = j, q, parts
            self.group = G // parts
            self.rows, self.toks = R // parts, T // parts
            self.buf = j if NCH == 1 else j * NCH + q
            if parts == 1:
                self.sem = 2 * self.buf
                self.span = pl.ds(0, R)
                self.first = 0 if LINE else q * R
            else:
                self.sem = 2 * j + q
                self.span = pl.ds(pl.multiple_of(q * self.rows, self.rows), self.rows)
                self.first = q * self.rows
            if not LINE:
                self.blocks = [q * G + i for i in range(G)]
            elif parts == 1:
                self.blocks = order
            else:
                self.blocks = [jnp.where(q == 0, e, fa), jnp.where(q == 0, nb, fb)]

        def pieces(self):
            if LINE and self.parts == 1:
                return [Item(self.j, 1, 2), Item(self.j, 0, 2)]
            return [self]

        def row(self, table):
            pairs = self.group // 2
            at = 0 if LINE and self.parts == 1 else self.q * pairs
            return jnp.concatenate(
                [table[at + p, pl.ds(self.j, 1), :] for p in range(pairs)], axis=1)

    def taken(it):
        row = it.row(slot_c)
        return (row.astype(jnp.int32) - it.first
                == lax.broadcasted_iota(jnp.int32, (it.rows, it.toks), 0))

    def pair_copy(it):
        return remote(s1.at[it.buf, :, it.span], r1.at[it.buf, :, it.span],
                      p_s, p_r.at[it.sem], dp=mate)

    def sum_copy(it, k):
        return remote(s2.at[it.buf, k - 1, it.span], r2.at[it.buf, k - 1, it.span],
                      q_s, q_r.at[it.sem, k], dp=2 * across(k) + c)

    def share_copy(it, k):
        return remote(hid.at[it.buf, d, it.span], hid.at[it.buf, d, it.span],
                      h_s, h_r.at[it.sem, k], dp=2 * across(k) + c)

    def mate_copy(it, k):
        block = 2 * source(k) + c
        return remote(hid.at[it.buf, block, it.span], hid.at[it.buf, block, it.span],
                      h_s, f_r.at[it.sem, k], dp=mate)

    def stage_a(it, first, last):
        j, span = it.j, it.span
        slot = lax.rem(j, NB)

        @pl.when(first)
        def _():
            for copy in w_gu(j, slot):
                copy.wait()

        pick = jnp.where(taken(it), 1.0, 0.0).astype(BF16)
        for at in range(0, width, ct):
            xq = jnp.concatenate([xall[b, :, at:at + ct] for b in it.blocks], axis=0)
            rows[:it.rows, at:at + ct] = dot(pick, xq).astype(BF16)

        def block(m, core):
            cols = pl.ds(pl.multiple_of((2 * m + core) * hb, hb), hb)
            xr = rows[:it.rows, :]
            return dot(xr, wg[slot, :, cols]), dot(xr, wu[slot, :, cols])

        for m in range(M):
            g, u = block(m, 1 - c)
            s1[it.buf, m, span, :hb] = g.astype(BF16)
            s1[it.buf, m, span, hb:] = u.astype(BF16)
        for piece in it.pieces():
            pair_copy(piece).start()
        for m in range(M):
            g, u = block(m, c)
            keep[it.buf, m, span, :hb] = g.astype(BF16)
            keep[it.buf, m, span, hb:] = u.astype(BF16)

        @pl.when(last & (j + NB < EL))
        def _():
            for copy in w_gu(j + NB, slot):
                copy.start()

    def stage_b(it):
        i, span = it.buf, it.span
        pair_copy(it).wait_recv()
        for k in range(1, M):
            to = across(k)
            s2[i, k - 1, span] = (keep[i, to, span].astype(F32)
                                  + r1[i, to, span].astype(F32)).astype(BF16)
            sum_copy(it, k).start()

    def stage_c(it):
        i, span = it.buf, it.span
        total = keep[i, x, span].astype(F32) + r1[i, x, span].astype(F32)
        for k in range(1, M):
            sum_copy(it, k).wait_recv()
            total = total + r2[i, k - 1, span].astype(F32)
        g, u = total[:, :hb], total[:, hb:]
        hid[i, d, span] = (g / (1.0 + jnp.exp(-g)) * u).astype(BF16)
        for k in range(1, M):
            share_copy(it, k).start()
        mate_copy(it, 0).start()

    def stage_d(it):
        for k in range(1, M):
            share_copy(it, k).wait_recv()
            mate_copy(it, k).start()

    def stage_e(it, first, last):
        j, span = it.j, it.span
        slot = lax.rem(j, ND)

        @pl.when(first)
        def _():
            w_d(j, slot).wait()

        for piece in it.pieces():
            for k in range(M):
                mate_copy(piece, k).wait_recv()
        hit = taken(it)
        scale = jnp.sum(jnp.where(hit, it.row(wgt_c), 0.0), axis=1, keepdims=True)
        pick = jnp.where(hit, 1.0, 0.0).astype(BF16)
        hidden = jnp.concatenate([hid[it.buf, b, span] for b in range(DP)], axis=1)
        for at in range(0, width, ct):
            out = (dot(hidden, wd[slot, :, at:at + ct]) * scale).astype(BF16)
            add = dot(pick, out, ((0,), (0,)))
            for i, b in enumerate(it.blocks):
                acc[b, :, at:at + ct] += add[i * tok:(i + 1) * tok]

        @pl.when(last & (j + ND < EL))
        def _():
            w_d(j + ND, slot).start()

    def tail(way, s, n, target):
        part = pl.ds(n * half, half)
        return remote(rs_s.at[s, part], rs_in.at[way, s, part],
                      t_s.at[s, n], t_r.at[way, s, n], expert=target)

    def pass_on(way, s, n, target, adds):
        part = pl.ds(n * half, half)
        if adds is None:
            rs_s[s, part] = acc[s, part].astype(BF16)
        else:
            @pl.when(adds)
            def _():
                tail(way, s, n, e).wait_recv()
                rs_s[s, part] = (acc[s, part] + rs_in[way, s, part].astype(F32)).astype(BF16)

            @pl.when(jnp.logical_not(adds))
            def _():
                rs_s[s, part] = acc[s, part].astype(BF16)
        tail(way, s, n, target).start()

    if LINE:
        B, C, D, L = LINE_LAGS[1:]

        def piece(t):
            far = (t >= K) & (t < 3 * K)
            j = t - jnp.where(t >= K, K, 0) - jnp.where(t >= 3 * K, K, 0)
            return Item(j, jnp.where(far, 1, 0), 2)

        def step(i, carry):
            @pl.when(i == K)
            def _():
                with jax.named_scope("gather3"):
                    @pl.when(jnp.logical_not(mid))
                    def _():
                        arrived(fa)
                        arrived(fb)

                    routing(fa, 1, 0)
                    routing(fb, 1, 1)

            @pl.when(i < 2 * K)
            def _():
                with jax.named_scope("stage_a"):
                    it = piece(i)
                    stage_a(it, i < K, i >= K)

            @pl.when((i >= 2 * K) & (i < 3 * K))
            def _():
                with jax.named_scope("stage_a"):
                    stage_a(Item(i - K, 0, 1), i >= 0, i >= 0)

            @pl.when(i == 0)
            def _():
                start_down()

            for n, parts in enumerate(((0, 1), (2,))):
                @pl.when((i == n) & mid)
                def _(parts=parts):
                    with jax.named_scope("gather2"):
                        arrived(fb, parts)
                        for copy in gather_to(fb, 1 - onward, 3 - fb, parts):
                            copy.start()

            for lag, stage in ((B, stage_b), (C, stage_c), (D, stage_d)):
                @pl.when((i >= lag) & (i < 4 * K + lag))
                def _(lag=lag, stage=stage):
                    with jax.named_scope(stage.__name__):
                        stage(piece(i - lag))

            t = i - L

            @pl.when((t >= K) & (t < 2 * K))
            def _():
                with jax.named_scope("stage_e"):
                    stage_e(Item(t - K, 0, 1), t >= 0, t >= 0)

            @pl.when(t >= 2 * K)
            def _():
                with jax.named_scope("stage_e"):
                    it = piece(t)
                    stage_e(it, t < 3 * K, t < 0)

            @pl.when((t == 3 * K - 1) & jnp.logical_not(mid))
            def _():
                with jax.named_scope("r0"):
                    for s in (fb, fa):
                        for n in range(2):
                            pass_on(onward, s, n, nb, None)

            for n in range(2):
                @pl.when((t == 4 * K - 3 + n) & mid)
                def _(n=n):
                    with jax.named_scope("r1"):
                        pass_on(onward, fb, n, nb, t >= 0)
            return carry

        lax.fori_loop(0, 4 * K + L, step, 0)

        with jax.named_scope("r2"):
            for n in range(2):
                pass_on(onward, nb, n, nb, mid)

            @pl.when(mid)
            def _():
                for n in range(2):
                    pass_on(1 - onward, fa, n, fa, e >= 0)
    else:
        stages = (lambda it: stage_a(it, first_of(it), last_of(it)), stage_b, stage_c, stage_d,
                  lambda it: stage_e(it, first_of(it), last_of(it)))

        def first_of(it):
            return it.q == 0

        def last_of(it):
            return it.q == NCH - 1

        def item(t):
            return Item(lax.div(t, NCH), lax.rem(t, NCH), 1)

        def step(i, carry):
            for stage, lag in zip(stages, LAGS):
                @pl.when((i >= lag) & (i < N + lag))
                def _(stage=stage, lag=lag):
                    stage(item(i - lag))
            return carry

        lax.fori_loop(0, N + LAGS[-1], step, 0)

        def tail_step(t, carry):
            far, near = E - 1 - t, t
            for n in range(2):
                @pl.when((far > e) & has_right)
                def _(n=n):
                    pass_on(0, far, n, e + 1, has_left)

                @pl.when((near < e) & has_left)
                def _(n=n):
                    pass_on(1, near, n, e - 1, has_right)
            return carry

        lax.fori_loop(0, E - 1, tail_step, 0)

    with jax.named_scope("drain"):
        def drain_line(s, carry):
            for p in range(3):
                @pl.when((s <= e) & has_right)
                def _(p=p):
                    gather_to(s, 0, e, (p,))[0].wait_send()

                @pl.when((s >= e) & has_left)
                def _(p=p):
                    gather_to(s, 1, e, (p,))[0].wait_send()
            return carry

        lax.fori_loop(0, E, drain_line, 0)
        remote(s1, r1, p_s, p_r.at[0], dp=mate).wait_send()
        remote(s2, r2, q_s, q_r.at[0, 1], dp=mate).wait_send()
        sent = hid.at[:, pl.ds(0, 2 * M - 1)]
        remote(sent, sent, h_s, h_r.at[0, 1], dp=mate).wait_send()

    with jax.named_scope("own"):
        for n in range(2):
            part = pl.ds(n * half, half)
            for way, has in ((0, has_left), (1, has_right)):
                @pl.when(has)
                def _(way=way):
                    tail(way, e, n, e).wait_recv()
                    acc[e, part] = acc[e, part] + rs_in[way, e, part].astype(F32)

            out_ref[part] = acc[e, part].astype(BF16)

        def drain_sums(s, carry):
            @pl.when(s != e)
            def _():
                for n in range(2):
                    tail(0, s, n, e).wait_send()
            return carry

        lax.fori_loop(0, E, drain_sums, 0)


def on_device(tokens, expert_ids, scores, w_gate, w_up, w_down):
    E, DP = lax.axis_size("expert"), lax.axis_size("dp")
    tok, width = tokens.shape
    top = expert_ids.shape[1]
    EL, _, H = w_gate.shape
    n_exp = E * EL
    CAP = 2 * tok * top // n_exp
    G = min(E, 4)
    NCH = E // G
    LINE = E == 4 and EL % 2 == 0 and EL >= 4
    NB = EL // 2 if LINE else min(3, EL)
    ND = EL // 2 + 2 if LINE else min(3, EL)
    ct = tile_of(width)
    M, hb, R, N = DP // 2, H // DP, G * CAP, EL * NCH
    EP = max(EL, 8)
    vmem, dma = pltpu.VMEM, pltpu.SemaphoreType.DMA
    scratch = [
        vmem((NB, width, H), BF16), vmem((NB, width, H), BF16), vmem((ND, H, width), BF16),
        vmem((E, tok, width), BF16), vmem((E, 2 * top, tok), F32),
        vmem((E // 2, EP, 2 * tok), F32), vmem((E // 2, EP, 2 * tok), F32),
        vmem((R, width), BF16),
        vmem((N, M, R, 2 * hb), BF16), vmem((N, M, R, 2 * hb), BF16),
        vmem((N, M, R, 2 * hb), BF16),
        vmem((N, M - 1, R, 2 * hb), BF16), vmem((N, M - 1, R, 2 * hb), BF16),
        vmem((N, DP, R, hb), BF16),
        vmem((E, tok, width), F32),
        vmem((E, tok, width), BF16), vmem((2, E, tok, width), BF16),
        dma((2, NB)), dma((ND,)), dma((2, 3, E)), dma((3, E)),
        dma(()), dma((2 * N,)), dma(()), dma((2 * N, M)), dma(()), dma((2 * N, M)),
        dma((2 * N, M)),
        dma((E, 2)), dma((2, E, 2)),
    ]
    whole = pl.BlockSpec(memory_space=pltpu.VMEM)
    hbm = pl.BlockSpec(memory_space=pl.ANY)
    return pl.pallas_call(
        functools.partial(kernel, (E, DP, EL, NCH, G, CAP, NB, ND, LINE, ct)),
        out_shape=jax.ShapeDtypeStruct((tok, width), BF16),
        in_specs=[whole] * 3 + [hbm] * 3,
        out_specs=whole,
        scratch_shapes=scratch,
        compiler_params=pltpu.CompilerParams(
            collective_id=0, has_side_effects=True, vmem_limit_bytes=62 * 2**20),
        name="routed_experts",
    )(tokens, expert_ids.T, scores.T, w_gate, w_up, w_down)


def solution(mesh):
    in_specs = (
        P(("groups", "expert"), "dp"),
        P(("groups", "expert"), None),
        P(("groups", "expert"), None),
        P("expert", "dp", None),
        P("expert", "dp", None),
        P("expert", None, "dp"),
    )
    out_specs = P(("groups", "expert"), "dp")
    return jax.shard_map(
        on_device, mesh=mesh, in_specs=in_specs, out_specs=out_specs, check_vma=False
    )
```

time: 87.1 us -> 71.2 us (0.82)
  Pallas kernels: 85.3 us -> 69.4 us
    pallas_call x1, Pallas kernels: 85.3 us -> 69.4 us  [on_device(): pl.pallas_call(functools.partial(kernel, (E, DP, EL, NCH, G, CAP, NB, ND,...]
where the time goes in v1:
time: 71.2 us; the launch traced here: 71.1 us
  Pallas kernels  69.4 us (97%)
  local copies, waits for them, and re-layouts  1.62 us (2%)
    pallas_call x1, Pallas kernels, on_device(): pl.pallas_call(functools.partial(kernel, (E, DP, EL, NCH, G, CAP, NB, ND,...  69.4 us
    unnamed x1, local copies, waits for them, and re-layouts  1.62 us

profile of v1, /device:TPU:0, one launch (start us, length us, event | category | flops | bytes accessed | tf_op | source)
XLA Modules:
  0.0 71.1 jit_solution(2781433045932764997)
XLA Ops:
  0.0 69.4 %routed_experts.1 = bf16[64,1536]{1,0:T(8,128)(2,1)} custom-call(bf16[64,1536]{1,0:T(8,128)(2,1)} %tok_ref.1, s32[8,64]{1,0:T(8,128)} %bitcast.2, f32[8,64]{1,0:T(8,128)} %bitcast.3, bf16[8,1536,1024]{2,1,0:T(8,128)(2,1)} %wg_hbm.1, bf16[8,1536,1024]{2,1,0:T(8,128)(2,1)} %wu_hbm.1, bf16[8,1024,1536]{2,1,0:T(8,128)(2,1)} %wd_hbm.1), custom_call_target="tpu_custom_call" | custom-call | tf_op jit(solution)/shard_map/routed_experts/pallas_call | solution.py:544
  69.5 1.6 %copy.8 = bf16[64,1536]{1,0:T(8,128)(2,1)} copy(bf16[64,1536]{1,0:T(8,128)(2,1)} %routed_experts.1) | data formatting | bytes 393216

commit v2 on v1

v2 whole, which is shorter than its diff:
```python
import functools

import jax
import jax.numpy as jnp
from jax import lax
from jax.experimental import pallas as pl
from jax.experimental.pallas import tpu as pltpu
from jax.sharding import PartitionSpec as P

MESH = pl.DeviceIdType.MESH
F32, BF16 = jnp.float32, jnp.bfloat16
LAGS = (0, 1, 3, 5, 7)
A, B, C, D, E, X = (32 * stage for stage in range(1, 7))
ORDER = (
    A, X, A + 1, X + 1, B, B + 1, A + 2, B + 2, A + 3, B + 3, C, C + 1, C + 2, X + 2, A + 4,
    C + 3, A + 5, B + 4, A + 6, B + 5, B + 6, A + 7, D, B + 7, D + 1, C + 4, A + 8, C + 5,
    D + 2, B + 8, C + 6, A + 9, C + 7, A + 10, B + 9, D + 3, D + 4, B + 10, A + 11, C + 8,
    D + 5, E, D + 6, B + 11, E + 1, D + 7, C + 9, C + 10, B + 12, E + 2, D + 8, E + 3, C + 11,
    D + 9, B + 13, E + 4, D + 10, B + 14, B + 15, E + 5, C + 12, D + 11, E + 6, E + 7, X + 3,
    C + 13, C + 14, C + 15, D + 12, D + 13, E + 8, X + 4, D + 14, D + 15, E + 9, E + 10, X + 5,
    E + 11,
)


def packed(codes):
    codes = codes + (0,) * (-len(codes) % 3)
    return [sum(code * 256 ** i for i, code in enumerate(codes[at:at + 3]))
            for at in range(0, len(codes), 3)]


def dot(a, b, dims=((1,), (0,))):
    return lax.dot_general(a, b, (dims, ((), ())), preferred_element_type=F32)


def remote(src, dst, send, recv, **where):
    return pltpu.make_async_remote_copy(
        src_ref=src, dst_ref=dst, send_sem=send, recv_sem=recv,
        device_id=where, device_id_type=MESH,
    )


def tile_of(size):
    for tile in (512, 384, 256, 128):
        if size % tile == 0:
            return tile
    return size


def kernel(dims, tok_hbm, ids_ref, sco_ref, wg_hbm, wu_hbm, wd_hbm, out_hbm,
           wg, wu, wd, xall, route, slot_c, wgt_c, rows, s1, r1, keep, s2, r2, hid, acc,
           rs_s, rs_in, out_v,
           io_sem, wsem, dsem, ag_s, ag_r, p_s, p_r, q_s, q_r, h_s, h_r, f_r, t_s, t_r):
    E, DP, EL, NCH, G, CAP, NB, ND, LINE, ct = dims
    M = DP // 2
    tok, width = tok_hbm.shape
    top = ids_ref.shape[0]
    H = wg.shape[2]
    hb = H // DP
    R, T = G * CAP, G * tok
    N = EL * NCH
    K = EL // 2
    half = tok // 2
    EP = slot_c.shape[1]
    e = lax.axis_index("expert")
    d = lax.axis_index("dp")
    x, c = lax.div(d, 2), lax.rem(d, 2)
    mate = 2 * x + 1 - c
    has_left, has_right = e > 0, e < E - 1
    if LINE:
        low = e < 2
        mid = (e == 1) | (e == 2)
        onward = jnp.where(low, 0, 1)
        nb = jnp.where(low, e + 1, e - 1)
        fb = jnp.where(low, 3, 0)
        fa = 6 - e - nb - fb
        order = (e, nb, fa, fb)

    def across(k):
        return lax.rem(x + k, M)

    def source(k):
        return lax.rem(x + M - k, M)

    def w_gu(j, slot):
        return (pltpu.make_async_copy(wg_hbm.at[j], wg.at[slot], wsem.at[0, slot]),
                pltpu.make_async_copy(wu_hbm.at[j], wu.at[slot], wsem.at[1, slot]))

    def w_d(j, slot):
        return pltpu.make_async_copy(wd_hbm.at[j], wd.at[slot], dsem.at[slot])

    def start_down():
        for j in range(ND):
            w_d(j, j).start()

    own_rows = pltpu.make_async_copy(tok_hbm, xall.at[e], io_sem.at[0])
    own_rows.start()
    def start_up(*experts):
        for j in experts:
            for copy in w_gu(j, j):
                copy.start()

    if not LINE:
        start_up(*range(NB))
        start_down()

    barrier = pltpu.get_barrier_semaphore()

    @pl.when(has_left)
    def _():
        pl.semaphore_signal(barrier, inc=1, device_id={"expert": e - 1}, device_id_type=MESH)

    @pl.when(has_right)
    def _():
        pl.semaphore_signal(barrier, inc=1, device_id={"expert": e + 1}, device_id_type=MESH)

    pl.semaphore_signal(barrier, inc=1, device_id={"dp": mate}, device_id_type=MESH)
    for k in range(1, M):
        pl.semaphore_signal(
            barrier, inc=1, device_id={"dp": 2 * across(k) + c}, device_id_type=MESH)

    route[e, :top] = ids_ref[...].astype(F32)
    route[e, top:] = sco_ref[...]

    def routing(block, pair, side):
        affinity = 1.0 / (1.0 + jnp.exp(-route[block, top:]))
        weights = 2.5 * affinity / jnp.sum(affinity, axis=0, keepdims=True)
        number = lax.broadcasted_iota(jnp.int32, (EP, tok), 0) + e * EL
        number = number.astype(F32)
        routed = jnp.zeros((EP, tok), F32)
        weight = jnp.zeros((EP, tok), F32)
        for k in range(top):
            hit = route[block, k:k + 1] == number
            routed = routed + jnp.where(hit, 1.0, 0.0)
            weight = weight + jnp.where(hit, weights[k:k + 1, :], 0.0)
        earlier = (lax.broadcasted_iota(jnp.int32, (tok, tok), 0)
                   < lax.broadcasted_iota(jnp.int32, (tok, tok), 1))
        rank = dot(routed.astype(BF16), jnp.where(earlier, 1.0, 0.0).astype(BF16))
        lanes = slice(side * tok, (side + 1) * tok)
        slot_c[pair, :, lanes] = jnp.where(routed > 0.5, rank + float(side * CAP), -float(R))
        wgt_c[pair, :, lanes] = weight

    acc[...] = jnp.zeros_like(acc)
    if LINE:
        routing(e, 0, 0)
    own_rows.wait()
    if LINE:
        start_up(0, 1)

    with jax.named_scope("barrierw"):
        pl.semaphore_wait(barrier, M + has_left.astype(jnp.int32) + has_right.astype(jnp.int32))

    def sent_sem(side, p, s):
        return ag_s.at[side, min(p, 1)] if LINE else ag_s.at[side, p, s]

    def gather_to(s, side, target, parts=(0, 1, 2)):
        copies = []
        for p in parts:
            ref = route.at[s] if p == 0 else xall.at[s, pl.ds((p - 1) * half, half)]
            copies.append(remote(ref, ref, sent_sem(side, p, s), ag_r.at[p, s], expert=target))
        return copies

    def start_right(s, parts=(0, 1, 2)):
        @pl.when(has_right)
        def _():
            for copy in gather_to(s, 0, e + 1, parts):
                copy.start()

    def start_left(s, parts=(0, 1, 2)):
        @pl.when(has_left)
        def _():
            for copy in gather_to(s, 1, e - 1, parts):
                copy.start()

    def gather_step(k, parts=(0, 1, 2)):
        @pl.when(e - k >= 0)
        def _():
            for copy in gather_to(e - k, 0, e, parts):
                copy.wait_recv()
            start_right(e - k, parts)

        @pl.when(e + k <= E - 1)
        def _():
            for copy in gather_to(e + k, 1, e, parts):
                copy.wait_recv()
            start_left(e + k, parts)

    def arrived(s, parts=(0, 1, 2)):
        for copy in gather_to(s, 0, e, parts):
            copy.wait_recv()

    for parts in ((0, 1), (2,)):
        start_right(e, parts)
        start_left(e, parts)

    if not LINE:
        def whole_step(k, carry):
            gather_step(k)
            return carry

        def list_pair(p, carry):
            routing(2 * p, p, 0)
            routing(2 * p + 1, p, 1)
            return carry

        lax.fori_loop(1, E, whole_step, 0)
        lax.fori_loop(0, E // 2, list_pair, 0)

    class Item:
        def __init__(self, j, pos, n, q=0):
            self.j, self.n, self.q = j, n, q
            self.rows, self.toks = n * CAP, n * tok
            self.buf = j * NCH + q
            self.sem = 2 * self.buf + (pos // 2 if isinstance(pos, int) else lax.div(pos, 2))
            start = pos * CAP if isinstance(pos, int) else pl.multiple_of(pos * CAP, n * CAP)
            self.span = pl.ds(start, self.rows)
            first = q * (G // 2) + (pos // 2 if isinstance(pos, int) else lax.div(pos, 2))
            self.pairs = [first + i for i in range(n // 2)]
            if not LINE:
                self.blocks = [q * G + i for i in range(n)]
            elif n == 4:
                self.blocks = order
            else:
                self.blocks = [jnp.where(pos == 0, e, fa), jnp.where(pos == 0, nb, fb)]

        def pieces(self):
            if not LINE or self.n < 4:
                return [self]
            return [Item(self.j, p, n) for p, n in self.cut]

        def row(self, table, step):
            return jnp.concatenate(
                [table[p, pl.ds(self.j, 1), :] + 2 * step * i
                 for i, p in enumerate(self.pairs)], axis=1)

    def taken(it):
        row = it.row(slot_c, float(CAP))
        return (row.astype(jnp.int32)
                == lax.broadcasted_iota(jnp.int32, (it.rows, it.toks), 0))

    def pair_copy(it):
        return remote(s1.at[it.buf, :, it.span], r1.at[it.buf, :, it.span],
                      p_s, p_r.at[it.sem], dp=mate)

    def sum_copy(it, k):
        return remote(s2.at[it.buf, k - 1, it.span], r2.at[it.buf, k - 1, it.span],
                      q_s, q_r.at[it.sem, k - 1], dp=2 * across(k) + c)

    def share_copy(it, k):
        return remote(hid.at[it.buf, d, it.span], hid.at[it.buf, d, it.span],
                      h_s, h_r.at[it.sem, k - 1], dp=2 * across(k) + c)

    def mate_copy(it, k):
        block = 2 * source(k) + c
        return remote(hid.at[it.buf, block, it.span], hid.at[it.buf, block, it.span],
                      h_s, f_r.at[it.sem], dp=mate)

    def stage_a(it, first, last):
        j, span = it.j, it.span
        slot = lax.rem(j, NB)

        pick = jnp.where(taken(it), 1.0, 0.0).astype(BF16)

        @pl.when(first)
        def _():
            for copy in w_gu(j, slot):
                copy.wait()

        for at in range(0, width, ct):
            xq = jnp.concatenate([xall[b, :, at:at + ct] for b in it.blocks], axis=0)
            rows[:it.rows, at:at + ct] = dot(pick, xq).astype(BF16)

        def block(m, core):
            cols = pl.ds(pl.multiple_of((2 * m + core) * hb, hb), hb)
            xr = rows[:it.rows, :]
            return dot(xr, wg[slot, :, cols]), dot(xr, wu[slot, :, cols])

        for m in range(M):
            g, u = block(m, 1 - c)
            s1[it.buf, m, span, :hb] = g.astype(BF16)
            s1[it.buf, m, span, hb:] = u.astype(BF16)
        for piece in it.pieces():
            pair_copy(piece).start()
        for m in range(M):
            g, u = block(m, c)
            keep[it.buf, m, span, :hb] = g.astype(BF16)
            keep[it.buf, m, span, hb:] = u.astype(BF16)

        @pl.when(last & (j + NB < EL))
        def _():
            for copy in w_gu(j + NB, slot):
                copy.start()

    def stage_b(it):
        i, span = it.buf, it.span
        pair_copy(it).wait_recv()
        for k in range(1, M):
            to = across(k)
            s2[i, k - 1, span] = (keep[i, to, span].astype(F32)
                                  + r1[i, to, span].astype(F32)).astype(BF16)
            sum_copy(it, k).start()

    def stage_c(it):
        i, span = it.buf, it.span
        total = keep[i, x, span].astype(F32) + r1[i, x, span].astype(F32)
        for k in range(1, M):
            sum_copy(it, k).wait_recv()
            total = total + r2[i, k - 1, span].astype(F32)
        g, u = total[:, :hb], total[:, hb:]
        hid[i, d, span] = (g / (1.0 + jnp.exp(-g)) * u).astype(BF16)
        for k in range(1, M):
            share_copy(it, k).start()
        mate_copy(it, 0).start()

    def stage_d(it):
        for k in range(1, M):
            share_copy(it, k).wait_recv()
            mate_copy(it, k).start()

    def stage_e(it, first, last):
        j, span = it.j, it.span
        slot = lax.rem(j, ND)
        hit = taken(it)
        scale = jnp.sum(jnp.where(hit, it.row(wgt_c, 0.0), 0.0), axis=1, keepdims=True)
        pick = jnp.where(hit, 1.0, 0.0).astype(BF16)

        @pl.when(first)
        def _():
            w_d(j, slot).wait()

        for piece in it.pieces():
            both = hid.at[it.buf, pl.ds(0, M), piece.span]
            remote(both, both, h_s, f_r.at[piece.sem], dp=mate).wait_recv()
        hidden = jnp.concatenate([hid[it.buf, b, span] for b in range(DP)], axis=1)

        def add_to(at, out):
            add = dot(pick, out, ((0,), (0,)))
            for i, b in enumerate(it.blocks):
                acc[b, :, at:at + ct] += add[i * tok:(i + 1) * tok]

        held = None
        for at in range(0, width, ct):
            out = (dot(hidden, wd[slot, :, at:at + ct]) * scale).astype(BF16)
            if held is not None:
                add_to(*held)
            held = (at, out)
        add_to(*held)

        @pl.when(last & (j + ND < EL))
        def _():
            w_d(j + ND, slot).start()

    def tail(at, s, n, target):
        part = pl.ds(n * half, half)
        return remote(rs_s.at[s, part], rs_in.at[at, part],
                      t_s if LINE else t_s.at[s, n], t_r.at[at, n], expert=target)

    def pass_on(to, s, n, target, have, adds):
        part = pl.ds(n * half, half)

        def alone():
            rs_s[s, part] = acc[s, part].astype(BF16)

        if adds is None:
            alone()
        else:
            pl.when(jnp.logical_not(adds))(alone)

            @pl.when(adds)
            def _():
                tail(have, s, n, e).wait_recv()
                rs_s[s, part] = (acc[s, part] + rs_in[have, part].astype(F32)).astype(BF16)

        tail(to, s, n, target).start()

    if LINE:
        with jax.named_scope("gather1"):
            gather_step(1, (0, 1))
            start_up(*range(2, NB))
            gather_step(1, (2,))
            routing(nb, 0, 1)

        def half_item(t):
            far = (t >= K) & (t < 3 * K)
            j = t - jnp.where(t >= K, K, 0) - jnp.where(t >= 3 * K, K, 0)
            return Item(j, jnp.where(far, 2, 0), 2)

        def full_item(j):
            it = Item(j, 0, 4)
            it.cut = ((2, 2), (0, 2))
            return it

        def run_a(u):
            @pl.when(u < 2 * K)
            def _():
                stage_a(half_item(u), u < K, u >= K)

            @pl.when(u >= 2 * K)
            def _():
                stage_a(full_item(u - K), u >= 0, u >= 0)

        def run_e(u):
            @pl.when(u < K)
            def _():
                stage_e(full_item(u), u >= 0, u >= 0)

            @pl.when(u >= K)
            def _():
                stage_e(half_item(u + K), u < 2 * K, u < 0)

        def event(u):
            for n, parts in enumerate(((0, 1), (2,))):
                @pl.when((u == n) & mid)
                def _(parts=parts):
                    arrived(fb, parts)
                    for copy in gather_to(fb, 1 - onward, 3 - fb, parts):
                        copy.start()

                @pl.when((u == 4 + n) & mid)
                def _(n=n):
                    pass_on(1, fb, n, fb, 0, u >= 0)

            @pl.when(u == 0)
            def _():
                start_down()

            @pl.when(u == 2)
            def _():
                @pl.when(jnp.logical_not(mid))
                def _():
                    arrived(fa)
                    arrived(fb)

                routing(fa, 1, 0)
                routing(fb, 1, 1)

            @pl.when((u == 3) & jnp.logical_not(mid))
            def _():
                for s, to in ((fb, 0), (fa, 2)):
                    for n in range(2):
                        pass_on(to, s, n, nb, None, None)

            @pl.when((u == 3) & mid)
            def _():
                for n in range(2):
                    pass_on(0, fa, n, fa, None, None)

        runs = (run_a, lambda t: stage_b(half_item(t)), lambda t: stage_c(half_item(t)),
                lambda t: stage_d(half_item(t)), run_e, event)
        words = packed(ORDER)

        def four(w, carry):
            word = jnp.int32(words[0])
            for i, value in enumerate(words[1:]):
                word = jnp.where(w == i + 1, value, word)

            def one(i, word):
                code = lax.rem(word, 256)
                stage, arg = lax.div(code, 32), lax.rem(code, 32)
                for i, run in enumerate(runs):
                    @pl.when(stage == i + 1)
                    def _(i=i, run=run):
                        with jax.named_scope("ABCDEX"[i]):
                            run(arg)
                return lax.div(word, 256)

            lax.fori_loop(0, 3, one, word)
            return carry

        lax.fori_loop(0, len(words), four, 0)

        with jax.named_scope("r2"):
            for n in range(2):
                pass_on(jnp.where(mid, 4, 3), nb, n, nb, 2, mid)
    else:
        stages = (lambda it: stage_a(it, first_of(it), last_of(it)), stage_b, stage_c, stage_d,
                  lambda it: stage_e(it, first_of(it), last_of(it)))

        def first_of(it):
            return it.q == 0

        def last_of(it):
            return it.q == NCH - 1

        def item(t):
            return Item(lax.div(t, NCH), 0, G, lax.rem(t, NCH))

        def step(i, carry):
            for stage, lag in zip(stages, LAGS):
                @pl.when((i >= lag) & (i < N + lag))
                def _(stage=stage, lag=lag):
                    stage(item(i - lag))
            return carry

        lax.fori_loop(0, N + LAGS[-1], step, 0)

        def tail_step(t, carry):
            far, near = E - 1 - t, t
            for n in range(2):
                @pl.when((far > e) & has_right)
                def _(n=n):
                    pass_on(far, far, n, e + 1, far, has_left)

                @pl.when((near < e) & has_left)
                def _(n=n):
                    pass_on(E + near, near, n, e - 1, E + near, has_right)
            return carry

        lax.fori_loop(0, E - 1, tail_step, 0)

    with jax.named_scope("drain"):
        if LINE:
            for side, has, count in ((0, has_right, e + 1), (1, has_left, E - e)):
                for n in range(1, E):
                    @pl.when(has & (count == n))
                    def _(side=side, n=n):
                        for p, ref in enumerate((route, xall)):
                            ref = ref.at[pl.ds(0, n)]
                            remote(ref, ref, ag_s.at[side, p], ag_r.at[p, 0], expert=e).wait_send()
        else:
            def drain_line(s, carry):
                for p in range(3):
                    @pl.when((s <= e) & has_right)
                    def _(p=p):
                        gather_to(s, 0, e, (p,))[0].wait_send()

                    @pl.when((s >= e) & has_left)
                    def _(p=p):
                        gather_to(s, 1, e, (p,))[0].wait_send()
                return carry

            lax.fori_loop(0, E, drain_line, 0)
        remote(s1, r1, p_s, p_r.at[0], dp=mate).wait_send()
        remote(s2, r2, q_s, q_r.at[0, 0], dp=mate).wait_send()
        sent = hid.at[:, pl.ds(0, 2 * M - 1)]
        remote(sent, sent, h_s, h_r.at[0, 0], dp=mate).wait_send()

    def result(n):
        part = pl.ds(n * half, half)
        return pltpu.make_async_copy(out_v.at[part], out_hbm.at[part], io_sem.at[n])

    with jax.named_scope("own"):
        for n in range(2):
            part = pl.ds(n * half, half)
            if LINE:
                total = acc[e, part]
                for at in (jnp.where(mid, 3, 0), jnp.where(mid, 4, 1)):
                    tail(at, e, n, e).wait_recv()
                    total = total + rs_in[at, part].astype(F32)
                out_v[part] = total.astype(BF16)
            else:
                for at, has in ((e, has_left), (E + e, has_right)):
                    @pl.when(has)
                    def _(at=at):
                        tail(at, e, n, e).wait_recv()
                        acc[e, part] = acc[e, part] + rs_in[at, part].astype(F32)

                out_v[part] = acc[e, part].astype(BF16)
            result(n).start()

        if LINE:
            three = rs_s.at[pl.ds(0, E - 1)]
            remote(three, three, t_s, t_r.at[0, 0], expert=e).wait_send()
        else:
            def drain_sums(s, carry):
                @pl.when(s != e)
                def _():
                    for n in range(2):
                        tail(s, s, n, e).wait_send()
                return carry

            lax.fori_loop(0, E, drain_sums, 0)
        for n in range(2):
            result(n).wait()


def on_device(tokens, expert_ids, scores, w_gate, w_up, w_down):
    E, DP = lax.axis_size("expert"), lax.axis_size("dp")
    tok, width = tokens.shape
    top = expert_ids.shape[1]
    EL, _, H = w_gate.shape
    n_exp = E * EL
    CAP = 2 * tok * top // n_exp
    G = min(E, 4)
    NCH = E // G
    LINE = E == 4 and EL == 8
    NB = EL // 2 if LINE else min(3, EL)
    ND = EL // 2 + 2 if LINE else min(3, EL)
    ct = tile_of(width)
    M, hb, R, N = DP // 2, H // DP, G * CAP, EL * NCH
    EP = max(EL, 8)
    vmem, dma = pltpu.VMEM, pltpu.SemaphoreType.DMA
    scratch = [
        vmem((NB, width, H), BF16), vmem((NB, width, H), BF16), vmem((ND, H, width), BF16),
        vmem((E, tok, width), BF16), vmem((E, 2 * top, tok), F32),
        vmem((E // 2, EP, 2 * tok), F32), vmem((E // 2, EP, 2 * tok), F32),
        vmem((R, width), BF16),
        vmem((N, M, R, 2 * hb), BF16), vmem((N, M, R, 2 * hb), BF16),
        vmem((N, M, R, 2 * hb), BF16),
        vmem((N, M - 1, R, 2 * hb), BF16), vmem((N, M - 1, R, 2 * hb), BF16),
        vmem((N, DP, R, hb), BF16),
        vmem((E, tok, width), F32),
        vmem((E, tok, width), BF16), vmem((5 if LINE else 2 * E, tok, width), BF16),
        vmem((tok, width), BF16),
        dma((2,)), dma((2, NB)), dma((ND,)), dma((2, 2) if LINE else (2, 3, E)), dma((3, E)),
        dma(()), dma((2 * N,)), dma(()), dma((2 * N, M - 1)), dma(()), dma((2 * N, M - 1)),
        dma((2 * N,)),
        dma(() if LINE else (E, 2)), dma((5 if LINE else 2 * E, 2)),
    ]
    whole = pl.BlockSpec(memory_space=pltpu.VMEM)
    hbm = pl.BlockSpec(memory_space=pl.ANY)
    return pl.pallas_call(
        functools.partial(kernel, (E, DP, EL, NCH, G, CAP, NB, ND, LINE, ct)),
        out_shape=jax.ShapeDtypeStruct((tok, width), BF16),
        in_specs=[hbm] + [whole] * 2 + [hbm] * 3,
        out_specs=hbm,
        scratch_shapes=scratch,
        compiler_params=pltpu.CompilerParams(
            collective_id=0, has_side_effects=True, vmem_limit_bytes=62 * 2**20),
        name="routed_experts",
    )(tokens, expert_ids.T, scores.T, w_gate, w_up, w_down)


def solution(mesh):
    in_specs = (
        P(("groups", "expert"), "dp"),
        P(("groups", "expert"), None),
        P(("groups", "expert"), None),
        P("expert", "dp", None),
        P("expert", "dp", None),
        P("expert", None, "dp"),
    )
    out_specs = P(("groups", "expert"), "dp")
    return jax.shard_map(
        on_device, mesh=mesh, in_specs=in_specs, out_specs=out_specs, check_vma=False
    )
```

time: 71.2 us -> 64.8 us (0.910); the launches traced: 71.1 us -> 63.6 us
  Pallas kernels: 69.4 us -> 61.9 us
    pallas_call x1, Pallas kernels: 69.4 us -> 61.9 us  [on_device(): pl.pallas_call(functools.partial(kernel, (E, DP, EL, NCH, G, CAP, NB, ND,...]
where the time goes in v2:
time: 64.8 us; the launch traced here: 63.6 us
  Pallas kernels  61.9 us (96%)
  local copies, waits for them, and re-layouts  1.62 us (2%)
    pallas_call x1, Pallas kernels, on_device(): pl.pallas_call(functools.partial(kernel, (E, DP, EL, NCH, G, CAP, NB, ND,...  61.9 us
    unnamed x1, local copies, waits for them, and re-layouts  1.62 us

profile of v2, /device:TPU:0, one launch (start us, length us, event | category | flops | bytes accessed | tf_op | source)
XLA Modules:
  0.0 63.6 jit_solution(3240773542939005076)
XLA Ops:
  0.0 61.9 %routed_experts.1 = bf16[64,1536]{1,0:T(8,128)(2,1)} custom-call(bf16[64,1536]{1,0:T(8,128)(2,1)} %tok_hbm.1, s32[8,64]{1,0:T(8,128)} %bitcast.2, f32[8,64]{1,0:T(8,128)} %bitcast.3, bf16[8,1536,1024]{2,1,0:T(8,128)(2,1)} %wg_hbm.1, bf16[8,1536,1024]{2,1,0:T(8,128)(2,1)} %wu_hbm.1, bf16[8,1024,1536]{2,1,0:T(8,128)(2,1)} %wd_hbm.1), custom_call_target="tpu_custom_call" | custom-call | tf_op jit(solution)/shard_map/routed_experts/pallas_call | solution.py:611
  62.0 1.6 %copy.8 = bf16[64,1536]{1,0:T(8,128)(2,1)} copy(bf16[64,1536]{1,0:T(8,128)(2,1)} %routed_experts.1) | data formatting | bytes 393216

commit v3 on v2

--- a/solution.py
+++ b/solution.py
@@ -10,22 +10,23 @@
 MESH = pl.DeviceIdType.MESH
 F32, BF16 = jnp.float32, jnp.bfloat16
 LAGS = (0, 1, 3, 5, 7)
-A, B, C, D, E, X = (32 * stage for stage in range(1, 7))
+A, E, X = 16, 32, 48
+B, C, D = 16, 32, 48
 ORDER = (
-    A, X, A + 1, X + 1, B, B + 1, A + 2, B + 2, A + 3, B + 3, C, C + 1, C + 2, X + 2, A + 4,
-    C + 3, A + 5, B + 4, A + 6, B + 5, B + 6, A + 7, D, B + 7, D + 1, C + 4, A + 8, C + 5,
-    D + 2, B + 8, C + 6, A + 9, C + 7, A + 10, B + 9, D + 3, D + 4, B + 10, A + 11, C + 8,
-    D + 5, E, D + 6, B + 11, E + 1, D + 7, C + 9, C + 10, B + 12, E + 2, D + 8, E + 3, C + 11,
-    D + 9, B + 13, E + 4, D + 10, B + 14, B + 15, E + 5, C + 12, D + 11, E + 6, E + 7, X + 3,
-    C + 13, C + 14, C + 15, D + 12, D + 13, E + 8, X + 4, D + 14, D + 15, E + 9, E + 10, X + 5,
-    E + 11,
+    (0, 0, 0, A), (0, 0, 0, X), (B, 0, 0, A + 1), (0, 0, 0, X + 1), (B + 1, 0, 0, A + 2),
+    (C, B + 2, 0, A + 3), (C + 1, B + 3, 0, X + 2), (0, 0, 0, A + 4), (C + 2, D, B + 4, A + 5),
+    (C + 3, D + 1, B + 5, A + 6), (C + 4, D + 2, B + 6, A + 7), (C + 5, D + 3, B + 7, A + 8),
+    (C + 6, D + 4, B + 8, A + 9), (C + 7, D + 5, B + 9, A + 10), (C + 8, D + 6, B + 10, A + 11),
+    (C + 9, D + 7, B + 11, 0), (B + 12, 0, 0, E), (C + 10, B + 13, 0, E + 1),
+    (D + 8, 0, 0, E + 2), (C + 11, B + 14, D + 9, E + 3), (B + 15, 0, 0, E + 4),
+    (D + 10, 0, 0, E + 5), (C + 12, D + 11, 0, E + 6), (C + 13, 0, 0, E + 7), (0, 0, 0, X + 3),
+    (C + 14, D + 12, 0, E + 8), (C + 15, D + 13, 0, E + 9), (0, 0, 0, X + 4),
+    (D + 14, 0, 0, E + 10), (D + 15, 0, 0, X + 5), (0, 0, 0, E + 11),
 )
 
 
-def packed(codes):
-    codes = codes + (0,) * (-len(codes) % 3)
-    return [sum(code * 256 ** i for i, code in enumerate(codes[at:at + 3]))
-            for at in range(0, len(codes), 3)]
+def packed(rows):
+    return [a + 64 * (b + 64 * (c + 64 * d)) for a, b, c, d in rows]
 
 
 def dot(a, b, dims=((1,), (0,))):
@@ -46,14 +47,14 @@
     return size
 
 
-def kernel(dims, tok_hbm, ids_ref, sco_ref, wg_hbm, wu_hbm, wd_hbm, out_hbm,
+def kernel(dims, tok_hbm, ids_hbm, sco_hbm, wg_hbm, wu_hbm, wd_hbm, out_ref,
            wg, wu, wd, xall, route, slot_c, wgt_c, rows, s1, r1, keep, s2, r2, hid, acc,
-           rs_s, rs_in, out_v,
+           rs_s, rs_in, ids_ref, sco_ref,
            io_sem, wsem, dsem, ag_s, ag_r, p_s, p_r, q_s, q_r, h_s, h_r, f_r, t_s, t_r):
     E, DP, EL, NCH, G, CAP, NB, ND, LINE, ct = dims
     M = DP // 2
     tok, width = tok_hbm.shape
-    top = ids_ref.shape[0]
+    top = ids_hbm.shape[0]
     H = wg.shape[2]
     hb = H // DP
     R, T = G * CAP, G * tok
@@ -94,6 +95,10 @@
 
     own_rows = pltpu.make_async_copy(tok_hbm, xall.at[e], io_sem.at[0])
     own_rows.start()
+    own_ids = pltpu.make_async_copy(ids_hbm, ids_ref, io_sem.at[1])
+    own_scores = pltpu.make_async_copy(sco_hbm, sco_ref, io_sem.at[2])
+    own_ids.start()
+    own_scores.start()
     def start_up(*experts):
         for j in experts:
             for copy in w_gu(j, j):
@@ -118,6 +123,9 @@
         pl.semaphore_signal(
             barrier, inc=1, device_id={"dp": 2 * across(k) + c}, device_id_type=MESH)
 
+    acc[...] = jnp.zeros_like(acc)
+    own_ids.wait()
+    own_scores.wait()
     route[e, :top] = ids_ref[...].astype(F32)
     route[e, top:] = sco_ref[...]
 
@@ -139,7 +147,6 @@
         slot_c[pair, :, lanes] = jnp.where(routed > 0.5, rank + float(side * CAP), -float(R))
         wgt_c[pair, :, lanes] = weight
 
-    acc[...] = jnp.zeros_like(acc)
     if LINE:
         routing(e, 0, 0)
     own_rows.wait()
@@ -444,29 +451,33 @@
                 for n in range(2):
                     pass_on(0, fa, n, fa, None, None)
 
-        runs = (run_a, lambda t: stage_b(half_item(t)), lambda t: stage_c(half_item(t)),
-                lambda t: stage_d(half_item(t)), run_e, event)
         words = packed(ORDER)
 
-        def four(w, carry):
+        def light(code):
+            for n, stage in enumerate((stage_b, stage_c, stage_d)):
+                @pl.when(lax.div(code, 16) == n + 1)
+                def _(n=n, stage=stage):
+                    with jax.named_scope("BCD"[n]):
+                        stage(half_item(lax.rem(code, 16)))
+
+        def heavy(code):
+            for n, run in enumerate((run_a, run_e, event)):
+                @pl.when(lax.div(code, 16) == n + 1)
+                def _(n=n, run=run):
+                    with jax.named_scope("AEX"[n]):
+                        run(lax.rem(code, 16))
+
+        def step(i, carry):
             word = jnp.int32(words[0])
-            for i, value in enumerate(words[1:]):
-                word = jnp.where(w == i + 1, value, word)
-
-            def one(i, word):
-                code = lax.rem(word, 256)
-                stage, arg = lax.div(code, 32), lax.rem(code, 32)
-                for i, run in enumerate(runs):
-                    @pl.when(stage == i + 1)
-                    def _(i=i, run=run):
-                        with jax.named_scope("ABCDEX"[i]):
-                            run(arg)
-                return lax.div(word, 256)
-
-            lax.fori_loop(0, 3, one, word)
+            for n, value in enumerate(words[1:]):
+                word = jnp.where(i == n + 1, value, word)
+            for n in range(3):
+                code = lax.rem(lax.div(word, 64 ** n), 64)
+                pl.when(code > 0)(functools.partial(light, code))
+            heavy(lax.div(word, 64 ** 3))
             return carry
 
-        lax.fori_loop(0, len(words), four, 0)
+        lax.fori_loop(0, len(words), step, 0)
 
         with jax.named_scope("r2"):
             for n in range(2):
@@ -534,10 +545,6 @@
         sent = hid.at[:, pl.ds(0, 2 * M - 1)]
         remote(sent, sent, h_s, h_r.at[0, 0], dp=mate).wait_send()
 
-    def result(n):
-        part = pl.ds(n * half, half)
-        return pltpu.make_async_copy(out_v.at[part], out_hbm.at[part], io_sem.at[n])
-
     with jax.named_scope("own"):
         for n in range(2):
             part = pl.ds(n * half, half)
@@ -546,7 +553,7 @@
                 for at in (jnp.where(mid, 3, 0), jnp.where(mid, 4, 1)):
                     tail(at, e, n, e).wait_recv()
                     total = total + rs_in[at, part].astype(F32)
-                out_v[part] = total.astype(BF16)
+                out_ref[part] = total.astype(BF16)
             else:
                 for at, has in ((e, has_left), (E + e, has_right)):
                     @pl.when(has)
@@ -554,8 +561,7 @@
                         tail(at, e, n, e).wait_recv()
                         acc[e, part] = acc[e, part] + rs_in[at, part].astype(F32)
 
-                out_v[part] = acc[e, part].astype(BF16)
-            result(n).start()
+                out_ref[part] = acc[e, part].astype(BF16)
 
         if LINE:
             three = rs_s.at[pl.ds(0, E - 1)]
@@ -569,8 +575,6 @@
                 return carry
 
             lax.fori_loop(0, E, drain_sums, 0)
-        for n in range(2):
-            result(n).wait()
 
 
 def on_device(tokens, expert_ids, scores, w_gate, w_up, w_down):
@@ -600,8 +604,8 @@
         vmem((N, DP, R, hb), BF16),
         vmem((E, tok, width), F32),
         vmem((E, tok, width), BF16), vmem((5 if LINE else 2 * E, tok, width), BF16),
-        vmem((tok, width), BF16),
-        dma((2,)), dma((2, NB)), dma((ND,)), dma((2, 2) if LINE else (2, 3, E)), dma((3, E)),
+        vmem((top, tok), jnp.int32), vmem((top, tok), F32),
+        dma((3,)), dma((2, NB)), dma((ND,)), dma((2, 2) if LINE else (2, 3, E)), dma((3, E)),
         dma(()), dma((2 * N,)), dma(()), dma((2 * N, M - 1)), dma(()), dma((2 * N, M - 1)),
         dma((2 * N,)),
         dma(() if LINE else (E, 2)), dma((5 if LINE else 2 * E, 2)),
@@ -610,9 +614,9 @@
     hbm = pl.BlockSpec(memory_space=pl.ANY)
     return pl.pallas_call(
         functools.partial(kernel, (E, DP, EL, NCH, G, CAP, NB, ND, LINE, ct)),
-        out_shape=jax.ShapeDtypeStruct((tok, width), BF16),
-        in_specs=[hbm] + [whole] * 2 + [hbm] * 3,
-        out_specs=hbm,
+        out_shape=pltpu.VMEM((tok, width), BF16),
+        in_specs=[hbm] * 6,
+        out_specs=whole,
         scratch_shapes=scratch,
         compiler_params=pltpu.CompilerParams(
             collective_id=0, has_side_effects=True, vmem_limit_bytes=62 * 2**20),

time: 64.8 us -> 62.5 us (0.965); the launches traced: 63.6 us -> 62 us
  local copies, waits for them, and re-layouts: 1.62 us -> 0.68 us
    unnamed x1, local copies, waits for them, and re-layouts: 1.62 us -> 0.68 us
where the time goes in v3:
time: 62.5 us; the launch traced here: 62 us
  Pallas kernels  61.4 us (98%)
  local copies, waits for them, and re-layouts  0.68 us (1%)
    pallas_call x1, Pallas kernels, on_device(): pl.pallas_call(functools.partial(kernel, (E, DP, EL, NCH, G, CAP, NB, ND,...  61.4 us

profile of v3, /device:TPU:0, one launch (start us, length us, event | category | flops | bytes accessed | tf_op | source)
XLA Modules:
  0.0 62.0 jit_solution(10224402078885920631)
XLA Ops:
  0.0 61.4 %routed_experts.1 = bf16[64,1536]{1,0:T(8,128)(2,1)S(1)} custom-call(bf16[64,1536]{1,0:T(8,128)(2,1)} %tok_hbm.1, s32[8,64]{1,0:T(8,128)} %bitcast.2, f32[8,64]{1,0:T(8,128)} %bitcast.3, bf16[8,1536,1024]{2,1,0:T(8,128)(2,1)} %wg_hbm.1, bf16[8,1536,1024]{2,1,0:T(8,128)(2,1)} %wu_hbm.1, bf16[8,1024,1536]{2,1,0:T(8,128)(2,1)} %wd_hbm.1), custom_call_target="tpu_custom_call" | custom-call | tf_op jit(solution)/shard_map/routed_experts/pallas_call | solution.py:615
  61.4 0.7 %copy.8 = bf16[64,1536]{1,0:T(8,128)(2,1)} copy(bf16[64,1536]{1,0:T(8,128)(2,1)S(1)} %routed_experts.1) | data formatting | bytes 393216

commit v4 on v3

--- a/solution.py
+++ b/solution.py
@@ -14,14 +14,15 @@
 B, C, D = 16, 32, 48
 ORDER = (
     (0, 0, 0, A), (0, 0, 0, X), (B, 0, 0, A + 1), (0, 0, 0, X + 1), (B + 1, 0, 0, A + 2),
-    (C, B + 2, 0, A + 3), (C + 1, B + 3, 0, X + 2), (0, 0, 0, A + 4), (C + 2, D, B + 4, A + 5),
-    (C + 3, D + 1, B + 5, A + 6), (C + 4, D + 2, B + 6, A + 7), (C + 5, D + 3, B + 7, A + 8),
-    (C + 6, D + 4, B + 8, A + 9), (C + 7, D + 5, B + 9, A + 10), (C + 8, D + 6, B + 10, A + 11),
-    (C + 9, D + 7, B + 11, 0), (B + 12, 0, 0, E), (C + 10, B + 13, 0, E + 1),
-    (D + 8, 0, 0, E + 2), (C + 11, B + 14, D + 9, E + 3), (B + 15, 0, 0, E + 4),
-    (D + 10, 0, 0, E + 5), (C + 12, D + 11, 0, E + 6), (C + 13, 0, 0, E + 7), (0, 0, 0, X + 3),
-    (C + 14, D + 12, 0, E + 8), (C + 15, D + 13, 0, E + 9), (0, 0, 0, X + 4),
-    (D + 14, 0, 0, E + 10), (D + 15, 0, 0, X + 5), (0, 0, 0, E + 11),
+    (B + 2, C, 0, A + 3), (B + 3, C + 1, 0, X + 2), (0, 0, 0, A + 4), (C + 2, B + 4, 0, A + 5),
+    (D, B + 5, C + 3, A + 6), (D + 1, B + 6, C + 4, A + 7), (D + 2, B + 7, 0, A + 8),
+    (C + 5, D + 3, B + 8, 0), (C + 6, 0, 0, A + 9), (D + 4, B + 9, 0, A + 10),
+    (C + 7, D + 5, B + 10, A + 11), (C + 8, D + 6, B + 11, E), (C + 9, 0, 0, E + 1),
+    (D + 7, B + 12, 0, E + 2), (C + 10, 0, 0, E + 3), (D + 8, C + 11, B + 13, 0),
+    (D + 9, 0, 0, E + 4), (C + 12, B + 14, D + 10, E + 5), (D + 11, B + 15, 0, E + 6),
+    (C + 13, 0, 0, E + 7), (0, 0, 0, X + 3), (C + 14, D + 12, C + 15, 0), (D + 13, 0, 0, E + 8),
+    (D + 14, 0, 0, E + 9), (0, 0, 0, X + 4), (D + 15, 0, 0, E + 10), (0, 0, 0, X + 5),
+    (0, 0, 0, E + 11),
 )
 
 

time: 62.5 us -> 61.5 us (0.984)
  Pallas kernels: 61.4 us -> 60.6 us
    pallas_call x1, Pallas kernels: 61.4 us -> 60.6 us  [on_device(): pl.pallas_call(functools.partial(kernel, (E, DP, EL, NCH, G, CAP, NB, ND,...]
where the time goes in v4:
time: 61.5 us; the launch traced here: 61.3 us
  Pallas kernels  60.6 us (99%)
  local copies, waits for them, and re-layouts  0.68 us (1%)
    pallas_call x1, Pallas kernels, on_device(): pl.pallas_call(functools.partial(kernel, (E, DP, EL, NCH, G, CAP, NB, ND,...  60.6 us

profile of v4, /device:TPU:0, one launch (start us, length us, event | category | flops | bytes accessed | tf_op | source)
XLA Modules:
  0.0 61.3 jit_solution(12272161009944067430)
XLA Ops:
  0.0 60.6 %routed_experts.1 = bf16[64,1536]{1,0:T(8,128)(2,1)S(1)} custom-call(bf16[64,1536]{1,0:T(8,128)(2,1)} %tok_hbm.1, s32[8,64]{1,0:T(8,128)} %bitcast.2, f32[8,64]{1,0:T(8,128)} %bitcast.3, bf16[8,1536,1024]{2,1,0:T(8,128)(2,1)} %wg_hbm.1, bf16[8,1536,1024]{2,1,0:T(8,128)(2,1)} %wu_hbm.1, bf16[8,1024,1536]{2,1,0:T(8,128)(2,1)} %wd_hbm.1), custom_call_target="tpu_custom_call" | custom-call | tf_op jit(solution)/shard_map/routed_experts/pallas_call | solution.py:616
  60.6 0.7 %copy.8 = bf16[64,1536]{1,0:T(8,128)(2,1)} copy(bf16[64,1536]{1,0:T(8,128)(2,1)S(1)} %routed_experts.1) | data formatting | bytes 393216

commit v5 on v4

--- a/solution.py
+++ b/solution.py
@@ -219,6 +219,7 @@
             self.rows, self.toks = n * CAP, n * tok
             self.buf = j * NCH + q
             self.sem = 2 * self.buf + (pos // 2 if isinstance(pos, int) else lax.div(pos, 2))
+            self.ring = lax.rem(j + 2 * pos, EL) if LINE else self.sem
             start = pos * CAP if isinstance(pos, int) else pl.multiple_of(pos * CAP, n * CAP)
             self.span = pl.ds(start, self.rows)
             first = q * (G // 2) + (pos // 2 if isinstance(pos, int) else lax.div(pos, 2))
@@ -247,15 +248,15 @@
 
     def pair_copy(it):
         return remote(s1.at[it.buf, :, it.span], r1.at[it.buf, :, it.span],
-                      p_s, p_r.at[it.sem], dp=mate)
+                      p_s, p_r.at[it.ring], dp=mate)
 
     def sum_copy(it, k):
         return remote(s2.at[it.buf, k - 1, it.span], r2.at[it.buf, k - 1, it.span],
-                      q_s, q_r.at[it.sem, k - 1], dp=2 * across(k) + c)
+                      q_s, q_r.at[it.ring, k - 1], dp=2 * across(k) + c)
 
     def share_copy(it, k):
         return remote(hid.at[it.buf, d, it.span], hid.at[it.buf, d, it.span],
-                      h_s, h_r.at[it.sem, k - 1], dp=2 * across(k) + c)
+                      h_s, h_r.at[it.ring, k - 1], dp=2 * across(k) + c)
 
     def mate_copy(it, k):
         block = 2 * source(k) + c
@@ -593,6 +594,7 @@
     ct = tile_of(width)
     M, hb, R, N = DP // 2, H // DP, G * CAP, EL * NCH
     EP = max(EL, 8)
+    NR = EL if LINE else 2 * N
     vmem, dma = pltpu.VMEM, pltpu.SemaphoreType.DMA
     scratch = [
         vmem((NB, width, H), BF16), vmem((NB, width, H), BF16), vmem((ND, H, width), BF16),
@@ -607,7 +609,7 @@
         vmem((E, tok, width), BF16), vmem((5 if LINE else 2 * E, tok, width), BF16),
         vmem((top, tok), jnp.int32), vmem((top, tok), F32),
         dma((3,)), dma((2, NB)), dma((ND,)), dma((2, 2) if LINE else (2, 3, E)), dma((3, E)),
-        dma(()), dma((2 * N,)), dma(()), dma((2 * N, M - 1)), dma(()), dma((2 * N, M - 1)),
+        dma(()), dma((NR,)), dma(()), dma((NR, M - 1)), dma(()), dma((NR, M - 1)),
         dma((2 * N,)),
         dma(() if LINE else (E, 2)), dma((5 if LINE else 2 * E, 2)),
     ]

time: 61.5 us -> 61.3 us (level)
  no operation moved by 1% of the time
where the time goes in v5:
time: 61.3 us; the launch traced here: 61.1 us
  Pallas kernels  60.4 us (99%)
  local copies, waits for them, and re-layouts  0.68 us (1%)
    pallas_call x1, Pallas kernels, on_device(): pl.pallas_call(functools.partial(kernel, (E, DP, EL, NCH, G, CAP, NB, ND,...  60.4 us

profile of v5, /device:TPU:0, one launch (start us, length us, event | category | flops | bytes accessed | tf_op | source)
XLA Modules:
  0.0 61.1 jit_solution(8366362821727278397)
XLA Ops:
  0.0 60.4 %routed_experts.1 = bf16[64,1536]{1,0:T(8,128)(2,1)S(1)} custom-call(bf16[64,1536]{1,0:T(8,128)(2,1)} %tok_hbm.1, s32[8,64]{1,0:T(8,128)} %bitcast.2, f32[8,64]{1,0:T(8,128)} %bitcast.3, bf16[8,1536,1024]{2,1,0:T(8,128)(2,1)} %wg_hbm.1, bf16[8,1536,1024]{2,1,0:T(8,128)(2,1)} %wu_hbm.1, bf16[8,1024,1536]{2,1,0:T(8,128)(2,1)} %wd_hbm.1), custom_call_target="tpu_custom_call" | custom-call | tf_op jit(solution)/shard_map/routed_experts/pallas_call | solution.py:618
  60.4 0.7 %copy.8 = bf16[64,1536]{1,0:T(8,128)(2,1)} copy(bf16[64,1536]{1,0:T(8,128)(2,1)S(1)} %routed_experts.1) | data formatting | bytes 393216
